TPU v7x, 32 devices: a whole 2x2x4 slice. The times are simulated.
32 devices in a mesh: lat: 4 (over y, core), lon: 8 (over z, x).
Axes of the slice: x: 2, y: 2, z: 4, core: 2. Of those that a mesh axis runs over, the one named last changes fastest.
Arguments:
- night_field: float32 [24, 256, 2048], P(None, 'lat', 'lon'), may hold values from -6 to 6
- lat_kernel: float32 [24, 5], replicated, may hold values from 0.1 to 1
- lon_kernel: float32 [24, 5], replicated, may hold values from 0.1 to 1
- damping: float32 [4, 24], replicated, may hold values from 0.2 to 0.8
- observed: float32 [24, 8192], P(None, ('lat', 'lon')), may hold values from -6 to 6
- pixel_slot: int32 [256, 2048], P('lat', 'lon'), may hold values from 0 to 63, as said below
- inbox_district: int32 [32, 64], P(('lat', 'lon')), may hold values from 0 to 255
Outputs:
- back_field: float32 [24, 256, 2048], P(None, 'lat', 'lon')
- residual: float32 [24, 8192], P(None, ('lat', 'lon'))
Inputs may be any that keep to these rules, and one draw needn't show every extreme that they name: `pixel_slot`: slot s of a device is sent to owner device s // 2, in the order latitude band first, then longitude strip. `inbox_district`: column source * 2 + k of an owner's row names the district, within the owner, of slot owner * 2 + k of that source device.
All inputs are finite; a program needn't handle non-finite values.
Results may differ from a plain program's by a relative error of at most 0.000068.
Values sent between devices are 32-bit elements; how exact they have to be, the bound alone decides.
A program may use at most 64 MiB of HBM per device.

v0:
```python
import functools

import jax
import jax.numpy as jnp
from jax import lax
from jax.experimental import pallas as pl
from jax.experimental.pallas import tpu as pltpu
from jax.sharding import PartitionSpec as P

CAP = 2
HALO = 8
LANES = 128
GROUP = 16
BLOCK = 4
HIGHEST = lax.Precision.HIGHEST
MESH = pl.DeviceIdType.MESH
F32 = jnp.float32
BF16 = jnp.bfloat16
NT = (((1,), (1,)), ((), ()))


def fill_taps(lat_ref, lon_ref, damp_ref, lonw, latw, lat_here, lat_count, adjoint):
    channels = lat_ref.shape[0]
    lat_taps = lat_ref[...] / jnp.sum(lat_ref[...], axis=1, keepdims=True)
    lon_taps = lon_ref[...] / jnp.sum(lon_ref[...], axis=1, keepdims=True)
    layers = damp_ref.shape[0]

    def column(values, index):
        return jnp.broadcast_to(values[:, index : index + 1], (channels, LANES))

    lon_cols = [column(lon_taps, 4 - b if adjoint else b) for b in range(5)]
    lat_cols = [column(lat_taps, 4 - a if adjoint else a) for a in range(5)]
    for b in range(5):
        lonw[b] = lon_cols[b] / lon_cols[2]
    eye = lax.broadcasted_iota(jnp.int32, (channels, channels), 0) == lax.broadcasted_iota(
        jnp.int32, (channels, channels), 1
    )
    for k in range(layers):
        layer = layers - 1 - k if adjoint else k
        rates = jnp.broadcast_to(damp_ref[layer : layer + 1, :], (channels, channels))
        rate = jnp.sum(jnp.where(eye, rates, 0.0), axis=1, keepdims=True)
        scale = jnp.broadcast_to(rate, (channels, LANES)) * lon_cols[2]
        for a in range(5):
            own = scale * lat_cols[a]
            mirrored = scale * lat_cols[4 - a]
            latw[k, 0, a] = jnp.where(lat_here == 0, mirrored, own)
            latw[k, 1, a] = own
            latw[k, 2, a] = jnp.where(lat_here == lat_count - 1, mirrored, own)


def filter_pass(src, dst, lonw, latw, k, rows, last, adjoint):
    ext_rows, channels, width = src.shape
    keep = width - LANES if last else width
    first = 2 * (k + 1)
    blocks = (ext_rows - 2 * first) // BLOCK

    def wide(tap):
        return jnp.concatenate([tap] * (keep // LANES), axis=1)

    def group(g, _):
        chans = pl.ds(pl.multiple_of(g * 8, 8), 8)
        lon_taps = [wide(lonw[b, chans, :]) for b in range(5)]

        def lon(row):
            v = src[row, chans, :]
            total = v[:, :keep]
            for b in (0, 1, 3, 4):
                total = total + lon_taps[b] * pltpu.roll(v, (2 - b) % width, 1)[:, :keep]
            return total

        def step(i, carry):
            top = first + i * BLOCK
            t = list(carry) + [lon(top + 2 + j) for j in range(BLOCK)]
            for j in range(BLOCK):
                row = top + j
                out = src[row, chans, :keep]
                for a in range(5):
                    which = row + (a - 2) if adjoint else row
                    region = (which >= HALO).astype(jnp.int32) + (which >= HALO + rows).astype(jnp.int32)
                    out = out - wide(latw[k, region, a, chans, :]) * t[j + a]
                dst[row, chans, :keep] = out
            return tuple(t[BLOCK:])

        lax.fori_loop(0, blocks, step, tuple(lon(first - 2 + j) for j in range(4)))
        return 0

    lax.fori_loop(0, channels // 8, group, 0)


def run_passes(bufs, lonw, latw, layers, rows, adjoint):
    for k in range(layers):
        filter_pass(bufs[k % 2], bufs[(k + 1) % 2], lonw, latw, k, rows, k == layers - 1, adjoint)
    return bufs[layers % 2]


def pieces(values):
    high = values.astype(BF16).astype(F32)
    rest = values - high
    middle = rest.astype(BF16).astype(F32)
    return high, middle, rest - middle


def stacked(values, height):
    gap = jnp.zeros((32 - values.shape[0], values.shape[1]), F32)
    high, middle, low = pieces(values)
    parts = [high, gap, middle, gap, low, gap]
    if height > 96:
        parts.append(jnp.zeros((height - 96, values.shape[1]), F32))
    return jnp.concatenate(parts, axis=0).astype(BF16)


def slot_ids(devices, width):
    place = lax.broadcasted_iota(jnp.int32, (CAP * devices, width), 0)
    return jnp.where(place < devices, CAP * place, CAP * (place - devices) + 1)


def one_hot(slot_row, ids):
    return jnp.where(jnp.broadcast_to(slot_row, ids.shape) == ids, 1.0, 0.0).astype(BF16)


def unpack_rows(buf, right_of, left_of, corners_of, lat_here, lat_count, rows):
    channels, width = buf.shape[1], buf.shape[2]
    base = width - LANES
    lane = lax.broadcasted_iota(jnp.int32, (channels, LANES), 1)

    def place(row, right, left, i_right, i_left):
        a = pltpu.roll(right, i_right, 1)
        b = pltpu.roll(left, i_left, 1)
        zero = jnp.zeros_like(a)
        buf[row, :, base:] = jnp.where(lane < HALO, a, jnp.where(lane >= LANES - HALO, b, zero))

    def tile(p, _):
        right, left = right_of(p), left_of(p)
        for i in range(GROUP):
            place(
                HALO + p * GROUP + i, right, left, (-HALO * i) % LANES, (LANES - HALO - HALO * i) % LANES
            )
        return 0

    lax.fori_loop(0, rows // GROUP, tile, 0)
    for v in range(2):
        polar = (lat_here == 0) if v == 0 else (lat_here == lat_count - 1)
        right, left = corners_of(v, 1), corners_of(v, 0)
        for e in range(HALO):
            if v == 0:
                i = jnp.where(polar, HALO - 1 - e, HALO + e)
            else:
                i = jnp.where(polar, GROUP - 1 - e, e)
            row = e if v == 0 else HALO + rows + e
            place(
                row, right, left, (LANES - HALO * i) % LANES, (2 * LANES - HALO - HALO * i) % LANES
            )


def forward_kernel(
    lat_count, lon_count,
    x_ref, lat_ref, lon_ref, damp_ref, obs_ref, slot_ref, inbox_ref,
    resid_ref, nb_ref, srows_ref, sstrip_ref, scorner_ref,
    buf_a, buf_b, lonw, latw, pack, st_rows, st_slots, st_strip, st_corner,
    send_a, recv_a, send_b, recv_b, padded,
    near_send, near_recv, a_send, a_recv, b_send, b_recv,
):
    devices = lat_count * lon_count
    channels, rows, cols = x_ref.shape
    layers = damp_ref.shape[0]
    la, lo = lax.axis_index("lat"), lax.axis_index("lon")
    me = la * lon_count + lo
    half = lon_count // 2

    def coords(index):
        return (index // lon_count, lax.rem(index, lon_count))

    barrier = pltpu.get_barrier_semaphore()

    def greet(i, _):
        pl.semaphore_signal(
            barrier, inc=1, device_id=coords(lax.rem(me + i, devices)), device_id_type=MESH
        )
        return 0

    lax.fori_loop(1, devices, greet, 0)

    def turn(j, _):
        block = x_ref[:, pl.ds(pl.multiple_of(j * 8, 8), 8), :]
        buf_a[pl.ds(HALO + j * 8, 8), :, 0:cols] = jnp.swapaxes(block, 0, 1)
        return 0

    lax.fori_loop(0, rows // 8, turn, 0)

    lane_c = lax.broadcasted_iota(jnp.int32, (channels + 8, LANES), 1)

    def pack_tile(p, _):
        low = jnp.zeros((channels + 8, LANES), F32)
        high = low
        for i in range(GROUP):
            row = p * GROUP + i
            field = buf_a[HALO + row, :, :]
            slots = slot_ref[pl.ds(row, 1), :].astype(F32)
            first = jnp.concatenate(
                [field[:, :LANES], jnp.broadcast_to(slots[:, :LANES], (8, LANES))], axis=0
            )
            final = jnp.concatenate(
                [field[:, cols - LANES : cols], jnp.broadcast_to(slots[:, cols - LANES :], (8, LANES))],
                axis=0,
            )
            here = (lane_c >= HALO * i) & (lane_c < HALO * (i + 1))
            low = jnp.where(here, pltpu.roll(first, HALO * i, 1), low)
            high = jnp.where(here, pltpu.roll(final, (HALO * (i + 1)) % LANES, 1), high)
        pack[0, p] = low
        pack[1, p] = high
        return 0

    lax.fori_loop(0, rows // GROUP, pack_tile, 0)
    tiles = rows // GROUP

    left = lax.rem(lo + lon_count - 1, lon_count)
    right = lax.rem(lo + 1, lon_count)
    far = lax.rem(lo + half, lon_count)
    far_left = lax.rem(lo + half + lon_count - 1, lon_count)
    far_right = lax.rem(lo + half + 1, lon_count)
    south, north = la == 0, la == lat_count - 1
    up_lat, up_slot = jnp.where(south, la, la - 1), jnp.where(south, 0, 1)
    down_lat, down_slot = jnp.where(north, la, la + 1), jnp.where(north, 1, 0)

    def near(index, src, dst, place, target):
        return pltpu.make_async_remote_copy(
            src_ref=src, dst_ref=dst, send_sem=near_send.at[index], recv_sem=near_recv.at[place],
            device_id=target, device_id_type=MESH,
        )

    copies = []
    for v, lat_to, slot_to, polar in ((0, up_lat, up_slot, south), (1, down_lat, down_slot, north)):
        start = 0 if v == 0 else rows - HALO
        mid = (lat_to, jnp.where(polar, far, lo))
        copies.append(near(v, buf_a.at[pl.ds(HALO + start, HALO), :, pl.ds(0, cols)],
                           st_rows.at[slot_to], slot_to, mid))
        copies.append(near(2 + v, slot_ref.at[pl.ds(start, HALO)], st_slots.at[slot_to], 2 + slot_to, mid))
        edge = 0 if v == 0 else tiles - 1
        for side in range(2):
            side_lon = jnp.where(polar, far_left, left) if side == 0 else jnp.where(polar, far_right, right)
            copies.append(near(6 + 2 * v + side, pack.at[side, edge], st_corner.at[slot_to, 1 - side],
                               6 + 2 * slot_to + (1 - side), (lat_to, side_lon)))
    for side in range(2):
        copies.append(near(4 + side, pack.at[side], st_strip.at[1 - side], 4 + (1 - side),
                           (la, left if side == 0 else right)))

    pl.semaphore_wait(barrier, devices - 1)
    for copy in copies:
        copy.start()

    fill_taps(lat_ref, lon_ref, damp_ref, lonw, latw, la, lat_count, False)

    somewhere = (la, right)
    for v in range(2):
        near(v, st_rows.at[v], st_rows.at[v], v, somewhere).wait_recv()
        near(2 + v, st_slots.at[v], st_slots.at[v], 2 + v, somewhere).wait_recv()
        near(4 + v, st_strip.at[v], st_strip.at[v], 4 + v, somewhere).wait_recv()
        for h in range(2):
            near(6 + 2 * v + h, st_corner.at[v, h], st_corner.at[v, h], 6 + 2 * v + h, somewhere).wait_recv()
    for copy in copies:
        copy.wait_send()

    def ghost(e, _):
        for v in range(2):
            polar = south if v == 0 else north
            row = jnp.where(polar, HALO - 1 - e, e)
            buf_a[e + v * (HALO + rows), :, 0:cols] = st_rows[v, row]
        return 0

    lax.fori_loop(0, HALO, ghost, 0)
    srows_ref[...] = st_slots[...]
    sstrip_ref[...] = st_strip[:, :, channels:, :]
    scorner_ref[...] = st_corner[:, :, channels:, :]
    unpack_rows(
        buf_a,
        lambda p: st_strip[1, p, 0:channels, :],
        lambda p: st_strip[0, p, 0:channels, :],
        lambda v, h: st_corner[v, h, 0:channels, :],
        la, lat_count, rows,
    )

    done = run_passes((buf_a, buf_b), lonw, latw, layers, rows, False)

    ids = slot_ids(devices, cols)

    def add_row(row, total):
        block = stacked(done[HALO + row, :, 0:cols], LANES)
        hot = one_hot(slot_ref[pl.ds(row, 1), :], ids)
        return total + lax.dot_general(hot, block, NT, preferred_element_type=F32)

    sums = lax.fori_loop(0, rows, add_row, jnp.zeros((CAP * devices, LANES), F32))
    sums = sums + pltpu.roll(sums, LANES - 32, 1) + pltpu.roll(sums, LANES - 64, 1)
    lane_d = lax.broadcasted_iota(jnp.int32, (devices, LANES), 1)
    sums = jnp.where(lane_d < 64, sums[:devices], pltpu.roll(sums[devices:], 64, 1))
    send_a[...] = sums.reshape(devices, 1, LANES)

    def hand_out(i, _):
        to = lax.rem(me + i, devices)
        pltpu.make_async_remote_copy(
            src_ref=send_a.at[to], dst_ref=recv_a.at[me], send_sem=a_send, recv_sem=a_recv,
            device_id=coords(to), device_id_type=MESH,
        ).start()
        return 0

    lax.fori_loop(1, devices, hand_out, 0)
    recv_a[pl.ds(me, 1)] = send_a[pl.ds(me, 1)]

    districts = obs_ref.shape[1]
    place = lax.broadcasted_iota(jnp.int32, (devices, CAP * devices), 1)
    source = lax.broadcasted_iota(jnp.int32, (devices, CAP * devices), 0)
    inbox = jnp.broadcast_to(inbox_ref[...], (devices, CAP * devices)).astype(F32)
    number = lax.broadcasted_iota(jnp.int32, (devices, districts), 1)
    tables = []
    for k in range(CAP):
        wanted = jnp.sum(jnp.where(place == CAP * source + k, inbox, 0.0), axis=1, keepdims=True)
        wanted = jnp.broadcast_to(wanted.astype(jnp.int32), (devices, districts))
        tables.append(jnp.where(wanted == number, 1.0, 0.0))

    others = pl.ds(0, devices - 1)
    whole_a = pltpu.make_async_remote_copy(
        src_ref=send_a.at[others], dst_ref=recv_a.at[others], send_sem=a_send, recv_sem=a_recv,
        device_id=somewhere, device_id_type=MESH,
    )
    whole_a.wait_recv()
    turned = recv_a[...].reshape(devices, LANES).T
    held = jnp.zeros((channels, districts), F32)
    for k in range(CAP):
        held = held + jnp.dot(
            turned[64 * k : 64 * k + channels], tables[k], precision=HIGHEST, preferred_element_type=F32
        )
    resid = held * ((districts / (rows * cols)) ** 0.5) - obs_ref[...]
    resid_ref[...] = resid

    give = jnp.zeros((devices, LANES), F32)
    for k in range(CAP):
        parts = [resid, jnp.zeros((LANES - channels - 64 * k, districts), F32)]
        if k > 0:
            parts = [jnp.zeros((64 * k, districts), F32)] + parts
        give = give + lax.dot_general(
            tables[k], jnp.concatenate(parts, axis=0), NT, precision=HIGHEST, preferred_element_type=F32
        )
    send_b[...] = give.reshape(devices, 1, LANES)
    for ea in range(lat_count + 2):
        for eb in range(lon_count + 2):
            real = min(max(ea - 1, 0), lat_count - 1)
            shift = half if real != ea - 1 else 0
            padded[ea, eb] = send_b[real * lon_count + (eb - 1 + shift) % lon_count]

    def hand_back(i, _):
        to = lax.rem(me + i, devices)
        a, b = coords(to)
        pltpu.make_async_remote_copy(
            src_ref=padded.at[pl.ds(a, 3), pl.ds(b, 3)], dst_ref=recv_b.at[me],
            send_sem=b_send, recv_sem=b_recv, device_id=(a, b), device_id_type=MESH,
        ).start()
        return 0

    lax.fori_loop(1, devices, hand_back, 0)
    recv_b[me] = padded[pl.ds(la, 3), pl.ds(lo, 3)]
    whole_b = pltpu.make_async_remote_copy(
        src_ref=recv_b.at[others], dst_ref=recv_b.at[others], send_sem=b_send, recv_sem=b_recv,
        device_id=somewhere, device_id_type=MESH,
    )
    whole_b.wait_recv()
    nb_ref[...] = recv_b[...]
    whole_a.wait_send()
    whole_b.wait_send()


def adjoint_kernel(
    lat_count, lon_count,
    nb_ref, srows_ref, sstrip_ref, scorner_ref, slot_ref, lat_ref, lon_ref, damp_ref, where_ref,
    out_ref,
    buf_a, buf_b, lonw, latw, mixers, strips, corners,
):
    devices = lat_count * lon_count
    channels, rows, cols = out_ref.shape
    layers = damp_ref.shape[0]
    la = where_ref[0]
    fill_taps(lat_ref, lon_ref, damp_ref, lonw, latw, la, lat_count, True)
    for v in range(3):
        for h in range(3):
            turned = nb_ref[:, v, h, 0, :].T
            wide = jnp.concatenate([turned[0:channels], turned[64 : 64 + channels]], axis=1)
            mixers[v, h] = stacked(wide, 96)

    def mix(mixer, hot):
        made = jnp.dot(mixer, hot, preferred_element_type=F32)
        return made[0:channels] + made[32 : 32 + channels] + made[64 : 64 + channels]

    ids_strip = slot_ids(devices, LANES)
    for h in range(2):
        for p in range(rows // GROUP):
            strips[h, p] = mix(mixers[1, 2 * h], one_hot(sstrip_ref[h, p, 0:1, :].astype(jnp.int32), ids_strip))
        for v in range(2):
            corners[v, h] = mix(
                mixers[2 * v, 2 * h], one_hot(scorner_ref[v, h, 0:1, :].astype(jnp.int32), ids_strip)
            )
    ids = slot_ids(devices, cols)

    def own(row, _):
        buf_a[HALO + row, :, 0:cols] = mix(mixers[1, 1], one_hot(slot_ref[pl.ds(row, 1), :], ids))
        return 0

    lax.fori_loop(0, rows, own, 0)

    def ghost(e, _):
        for v in range(2):
            polar = (la == 0) if v == 0 else (la == lat_count - 1)
            row = jnp.where(polar, HALO - 1 - e, e)
            buf_a[e + v * (HALO + rows), :, 0:cols] = mix(
                mixers[2 * v, 1], one_hot(srows_ref[v, pl.ds(row, 1), :], ids)
            )
        return 0

    lax.fori_loop(0, HALO, ghost, 0)
    unpack_rows(
        buf_a, lambda p: strips[1, p], lambda p: strips[0, p], lambda v, h: corners[v, h],
        la, lat_count, rows,
    )
    done = run_passes((buf_a, buf_b), lonw, latw, layers, rows, True)

    def turn(j, _):
        block = done[pl.ds(HALO + j * 8, 8), :, 0:cols]
        out_ref[:, pl.ds(pl.multiple_of(j * 8, 8), 8), :] = jnp.swapaxes(block, 0, 1)
        return 0

    lax.fori_loop(0, rows // 8, turn, 0)


def local(night_field, lat_kernel, lon_kernel, damping, observed, pixel_slot, inbox_district):
    channels, rows, cols = night_field.shape
    layers = damping.shape[0]
    lat_count, lon_count = lax.axis_size("lat"), lax.axis_size("lon")
    devices = lat_count * lon_count
    districts = observed.shape[1]
    tiles = rows // GROUP
    ext = (rows + 2 * HALO, channels, cols + LANES)
    vmem = pl.BlockSpec(memory_space=pltpu.VMEM)
    shape = jax.ShapeDtypeStruct
    taps = [pltpu.VMEM((5, channels, LANES), F32), pltpu.VMEM((layers, 3, 5, channels, LANES), F32)]
    sem = pltpu.SemaphoreType.DMA
    residual, nb, srows, sstrip, scorner = pl.pallas_call(
        functools.partial(forward_kernel, lat_count, lon_count),
        out_shape=(
            shape((channels, districts), F32),
            shape((devices, 3, 3, 1, LANES), F32),
            shape((2, HALO, cols), jnp.int32),
            shape((2, tiles, 8, LANES), F32),
            shape((2, 2, 8, LANES), F32),
        ),
        in_specs=[vmem] * 7,
        out_specs=(vmem,) * 5,
        scratch_shapes=[
            pltpu.VMEM(ext, F32),
            pltpu.VMEM(ext, F32),
            *taps,
            pltpu.VMEM((2, tiles, channels + 8, LANES), F32),
            pltpu.VMEM((2, HALO, channels, cols), F32),
            pltpu.VMEM((2, HALO, cols), jnp.int32),
            pltpu.VMEM((2, tiles, channels + 8, LANES), F32),
            pltpu.VMEM((2, 2, channels + 8, LANES), F32),
            pltpu.VMEM((devices, 1, LANES), F32),
            pltpu.VMEM((devices, 1, LANES), F32),
            pltpu.VMEM((devices, 1, LANES), F32),
            pltpu.VMEM((devices, 3, 3, 1, LANES), F32),
            pltpu.VMEM((lat_count + 2, lon_count + 2, 1, LANES), F32),
            sem((10,)), sem((10,)), sem, sem, sem, sem,
        ],
        compiler_params=pltpu.CompilerParams(collective_id=0, has_side_effects=True),
    )(night_field, lat_kernel, lon_kernel, damping, observed, pixel_slot, inbox_district)
    here = lax.axis_index("lat").reshape(1).astype(jnp.int32)
    back_field = pl.pallas_call(
        functools.partial(adjoint_kernel, lat_count, lon_count),
        out_shape=shape((channels, rows, cols), F32),
        in_specs=[vmem] * 8 + [pl.BlockSpec(memory_space=pltpu.SMEM)],
        out_specs=vmem,
        scratch_shapes=[
            pltpu.VMEM(ext, F32),
            pltpu.VMEM(ext, F32),
            *taps,
            pltpu.VMEM((3, 3, 96, CAP * devices), BF16),
            pltpu.VMEM((2, tiles, channels, LANES), F32),
            pltpu.VMEM((2, 2, channels, LANES), F32),
        ],
    )(nb, srows, sstrip, scorner, pixel_slot, lat_kernel, lon_kernel, damping, here)
    return back_field, residual


def solution(mesh):
    placed = (
        P(None, "lat", "lon"),
        P(),
        P(),
        P(),
        P(None, ("lat", "lon")),
        P("lat", "lon"),
        P(("lat", "lon"), None),
    )
    return jax.shard_map(
        local,
        mesh=mesh,
        in_specs=placed,
        out_specs=(P(None, "lat", "lon"), P(None, ("lat", "lon"))),
        check_vma=False,
    )
```

profile of v0, /device:TPU:0, one launch (start us, length us, event | category | flops | bytes accessed | tf_op | source)
XLA Modules:
  0.0 111.3 jit_solution(7958753802864162007)
XLA Ops:
  0.6 1.4 %copy.9.lat_ref = f32[24,5]{1,0:T(8,128)} copy(f32[24,5]{0,1:T(8,128)} %param.8) | data formatting | bytes 960 | tf_op args[1]
  2.0 1.4 %copy.10.lon_ref = f32[24,5]{1,0:T(8,128)} copy(f32[24,5]{0,1:T(8,128)} %param.9) | data formatting | bytes 960 | tf_op args[2]
  3.4 66.2 %shard_map.86 = (f32[24,256]{1,0:T(8,128)}, f32[32,3,3,1,128]{4,3,2,1,0:T(1,128)}, s32[2,8,256]{2,1,0:T(8,128)}, f32[2,4,8,128]{3,2,1,0:T(8,128)}, f32[2,2,8,128]{3,2,1,0:T(8,128)}) custom-call(f32[24,64,256]{2,1,0:T(8,128)} %x_ref.1, f32[24,5]{1,0:T(8,128)} %copy.9.lat_ref, f32[24,5]{1,0:T(8,128)} %copy.10.lon_ref, f32[4,24]{1,0:T(4,128)} %damp_ref.3, ...), custom_call_target="tpu_custom_call" | custom-call | tf_op jit(solution)/shard_map/pallas_call | solution.py:443
  69.5 0.0 copy-start
  69.5 41.2 %shard_map.87 = f32[24,64,256]{2,1,0:T(8,128)} custom-call(f32[32,3,3,1,128]{4,3,2,1,0:T(1,128)} %get-tuple-element.7.nb_ref, s32[2,8,256]{2,1,0:T(8,128)} %get-tuple-element.8.srows_ref, f32[2,4,8,128]{3,2,1,0:T(8,128)} %get-tuple-element.9.sstrip_ref, f32[2,2,8,128]{3,2,1,0:T(8,128)} %get-tuple-element.10.scorner_ref, s32[64,256]{1,0:T(8,128)} %slot_ref.3, ...), custom_call_target="tpu_custom_call" | custom-call | tf_op jit(solution)/shard_map/pallas_call | solution.py:473
  110.7 0.0 copy-done
  110.7 0.6 copy.14
Async XLA Ops:
  69.5 41.2 %copy-start = (f32[24,256]{1,0:T(8,128)S(1)}, f32[24,256]{1,0:T(8,128)}, u32[]{:S(2)}) copy-start(f32[24,256]{1,0:T(8,128)} %get-tuple-element.15) | copy-start | bytes 73732
where the time goes:
time: 112 us; the launch traced here: 111 us
  Pallas kernels  107 us (96%)
  local copies, waits for them, and re-layouts  3.34 us (3%)
    pallas_call x1, Pallas kernels, local(): pl.pallas_call(functools.partial(forward_kernel, lat_count, lon_count), o...  66.2 us
    pallas_call x1, Pallas kernels, local(): pl.pallas_call(functools.partial(adjoint_kernel, lat_count, lon_count), o...  41.2 us
    unnamed x5, local copies, waits for them, and re-layouts  3.34 us

commit v1 on v0

--- a/solution.py
+++ b/solution.py
@@ -20,26 +20,26 @@
 
 
 def fill_taps(lat_ref, lon_ref, damp_ref, lonw, latw, lat_here, lat_count, adjoint):
-    channels = lat_ref.shape[0]
-    lat_taps = lat_ref[...] / jnp.sum(lat_ref[...], axis=1, keepdims=True)
-    lon_taps = lon_ref[...] / jnp.sum(lon_ref[...], axis=1, keepdims=True)
+    channels = lat_ref.shape[1]
+    lat_taps = lat_ref[...] / jnp.sum(lat_ref[...], axis=0, keepdims=True)
+    lon_taps = lon_ref[...] / jnp.sum(lon_ref[...], axis=0, keepdims=True)
     layers = damp_ref.shape[0]
+    eye = lax.broadcasted_iota(jnp.int32, (channels, channels), 0) == lax.broadcasted_iota(
+        jnp.int32, (channels, channels), 1
+    )
 
     def column(values, index):
-        return jnp.broadcast_to(values[:, index : index + 1], (channels, LANES))
+        wide = jnp.broadcast_to(values[index : index + 1, :], (channels, channels))
+        tall = jnp.sum(jnp.where(eye, wide, 0.0), axis=1, keepdims=True)
+        return jnp.broadcast_to(tall, (channels, LANES))
 
     lon_cols = [column(lon_taps, 4 - b if adjoint else b) for b in range(5)]
     lat_cols = [column(lat_taps, 4 - a if adjoint else a) for a in range(5)]
     for b in range(5):
         lonw[b] = lon_cols[b] / lon_cols[2]
-    eye = lax.broadcasted_iota(jnp.int32, (channels, channels), 0) == lax.broadcasted_iota(
-        jnp.int32, (channels, channels), 1
-    )
+    damping = damp_ref[...]
     for k in range(layers):
-        layer = layers - 1 - k if adjoint else k
-        rates = jnp.broadcast_to(damp_ref[layer : layer + 1, :], (channels, channels))
-        rate = jnp.sum(jnp.where(eye, rates, 0.0), axis=1, keepdims=True)
-        scale = jnp.broadcast_to(rate, (channels, LANES)) * lon_cols[2]
+        scale = column(damping, layers - 1 - k if adjoint else k) * lon_cols[2]
         for a in range(5):
             own = scale * lat_cols[a]
             mirrored = scale * lat_cols[4 - a]
@@ -48,48 +48,79 @@
             latw[k, 2, a] = jnp.where(lat_here == lat_count - 1, mirrored, own)
 
 
-def filter_pass(src, dst, lonw, latw, k, rows, last, adjoint):
+def filter_pass(src, dst, tbufs, lonw, latw, k, rows, last, adjoint):
     ext_rows, channels, width = src.shape
-    keep = width - LANES if last else width
+    ring = width // LANES
+    kept = ring - 1 if last else ring
     first = 2 * (k + 1)
     blocks = (ext_rows - 2 * first) // BLOCK
-
-    def wide(tap):
-        return jnp.concatenate([tap] * (keep // LANES), axis=1)
-
-    def group(g, _):
-        chans = pl.ds(pl.multiple_of(g * 8, 8), 8)
-        lon_taps = [wide(lonw[b, chans, :]) for b in range(5)]
-
-        def lon(row):
-            v = src[row, chans, :]
-            total = v[:, :keep]
+    lane = lax.broadcasted_iota(jnp.int32, (8, LANES), 1)
+    groups = range(channels // 8)
+
+    def lane_tile(n):
+        return pl.ds(n * LANES, LANES)
+
+    def lon(row, g):
+        chans = pl.ds(g * 8, 8)
+        v = [src[row, chans, lane_tile(n)] for n in range(ring)]
+        totals = []
+        for n in range(kept):
+            before, after = v[(n - 1) % ring], v[(n + 1) % ring]
+            total = v[n]
             for b in (0, 1, 3, 4):
-                total = total + lon_taps[b] * pltpu.roll(v, (2 - b) % width, 1)[:, :keep]
-            return total
-
-        def step(i, carry):
-            top = first + i * BLOCK
-            t = list(carry) + [lon(top + 2 + j) for j in range(BLOCK)]
+                shift = 2 - b
+                if shift > 0:
+                    joined = jnp.where(lane >= LANES - shift, before, v[n])
+                else:
+                    joined = jnp.where(lane < -shift, after, v[n])
+                total = total + lonw[b, chans, :] * pltpu.roll(joined, shift % LANES, 1)
+            totals.append(total)
+        return totals
+
+    def keep_lon(row, g, totals):
+        for n, total in enumerate(totals):
+            tbufs[g][row, :, lane_tile(n)] = total
+
+    def lat(top, g):
+        chans = pl.ds(g * 8, 8)
+        t = [[tbufs[g][top - 2 + j, :, lane_tile(n)] for n in range(kept)] for j in range(BLOCK + 4)]
+        for j in range(BLOCK):
+            row = top + j
+            out = [src[row, chans, lane_tile(n)] for n in range(kept)]
+            for a in range(5):
+                which = row + (a - 2) if adjoint else row
+                region = (which >= HALO) * 1 + (which >= HALO + rows) * 1
+                tap = latw[k, region, a, chans, :]
+                out = [out[n] - tap * t[j + a][n] for n in range(kept)]
+            for n in range(kept):
+                dst[row, chans, lane_tile(n)] = out[n]
+
+    def begin(i, _):
+        for g in groups:
             for j in range(BLOCK):
-                row = top + j
-                out = src[row, chans, :keep]
-                for a in range(5):
-                    which = row + (a - 2) if adjoint else row
-                    region = (which >= HALO).astype(jnp.int32) + (which >= HALO + rows).astype(jnp.int32)
-                    out = out - wide(latw[k, region, a, chans, :]) * t[j + a]
-                dst[row, chans, :keep] = out
-            return tuple(t[BLOCK:])
-
-        lax.fori_loop(0, blocks, step, tuple(lon(first - 2 + j) for j in range(4)))
-        return 0
-
-    lax.fori_loop(0, channels // 8, group, 0)
-
-
-def run_passes(bufs, lonw, latw, layers, rows, adjoint):
+                row = first - 2 + i * BLOCK + j
+                keep_lon(row, g, lon(row, g))
+        return 0
+
+    lax.fori_loop(0, 2, begin, 0)
+
+    def step(i, _):
+        top = first + i * BLOCK
+        for g in groups:
+            ahead = [lon(top + BLOCK + 2 + j, g) for j in range(BLOCK)]
+            lat(top, g)
+            for j in range(BLOCK):
+                keep_lon(top + BLOCK + 2 + j, g, ahead[j])
+        return 0
+
+    lax.fori_loop(0, blocks - 1, step, 0)
+    for g in groups:
+        lat(first + (blocks - 1) * BLOCK, g)
+
+
+def run_passes(bufs, tbufs, lonw, latw, layers, rows, adjoint):
     for k in range(layers):
-        filter_pass(bufs[k % 2], bufs[(k + 1) % 2], lonw, latw, k, rows, k == layers - 1, adjoint)
+        filter_pass(bufs[k % 2], bufs[(k + 1) % 2], tbufs, lonw, latw, k, rows, k == layers - 1, adjoint)
     return bufs[layers % 2]
 
 
@@ -156,7 +187,7 @@
     lat_count, lon_count,
     x_ref, lat_ref, lon_ref, damp_ref, obs_ref, slot_ref, inbox_ref,
     resid_ref, nb_ref, srows_ref, sstrip_ref, scorner_ref,
-    buf_a, buf_b, lonw, latw, pack, st_rows, st_slots, st_strip, st_corner,
+    buf_a, buf_b, tbuf_0, tbuf_1, tbuf_2, lonw, latw, pack, st_rows, st_slots, st_strip, st_corner,
     send_a, recv_a, send_b, recv_b, padded,
     near_send, near_recv, a_send, a_recv, b_send, b_recv,
 ):
@@ -279,7 +310,7 @@
         la, lat_count, rows,
     )
 
-    done = run_passes((buf_a, buf_b), lonw, latw, layers, rows, False)
+    done = run_passes((buf_a, buf_b), (tbuf_0, tbuf_1, tbuf_2), lonw, latw, layers, rows, False)
 
     ids = slot_ids(devices, cols)
 
@@ -371,7 +402,7 @@
     lat_count, lon_count,
     nb_ref, srows_ref, sstrip_ref, scorner_ref, slot_ref, lat_ref, lon_ref, damp_ref, where_ref,
     out_ref,
-    buf_a, buf_b, lonw, latw, mixers, strips, corners,
+    buf_a, buf_b, tbuf_0, tbuf_1, tbuf_2, lonw, latw, mixers, strips, corners,
 ):
     devices = lat_count * lon_count
     channels, rows, cols = out_ref.shape
@@ -418,7 +449,7 @@
         buf_a, lambda p: strips[1, p], lambda p: strips[0, p], lambda v, h: corners[v, h],
         la, lat_count, rows,
     )
-    done = run_passes((buf_a, buf_b), lonw, latw, layers, rows, True)
+    done = run_passes((buf_a, buf_b), (tbuf_0, tbuf_1, tbuf_2), lonw, latw, layers, rows, True)
 
     def turn(j, _):
         block = done[pl.ds(HALO + j * 8, 8), :, 0:cols]
@@ -436,6 +467,7 @@
     districts = observed.shape[1]
     tiles = rows // GROUP
     ext = (rows + 2 * HALO, channels, cols + LANES)
+    sums = [pltpu.VMEM((ext[0], 8, ext[2]), F32)] * 3
     vmem = pl.BlockSpec(memory_space=pltpu.VMEM)
     shape = jax.ShapeDtypeStruct
     taps = [pltpu.VMEM((5, channels, LANES), F32), pltpu.VMEM((layers, 3, 5, channels, LANES), F32)]
@@ -454,6 +486,7 @@
         scratch_shapes=[
             pltpu.VMEM(ext, F32),
             pltpu.VMEM(ext, F32),
+            *sums,
             *taps,
             pltpu.VMEM((2, tiles, channels + 8, LANES), F32),
             pltpu.VMEM((2, HALO, channels, cols), F32),
@@ -468,7 +501,7 @@
             sem((10,)), sem((10,)), sem, sem, sem, sem,
         ],
         compiler_params=pltpu.CompilerParams(collective_id=0, has_side_effects=True),
-    )(night_field, lat_kernel, lon_kernel, damping, observed, pixel_slot, inbox_district)
+    )(night_field, lat_kernel.T, lon_kernel.T, damping, observed, pixel_slot, inbox_district)
     here = lax.axis_index("lat").reshape(1).astype(jnp.int32)
     back_field = pl.pallas_call(
         functools.partial(adjoint_kernel, lat_count, lon_count),
@@ -478,12 +511,13 @@
         scratch_shapes=[
             pltpu.VMEM(ext, F32),
             pltpu.VMEM(ext, F32),
+            *sums,
             *taps,
             pltpu.VMEM((3, 3, 96, CAP * devices), BF16),
             pltpu.VMEM((2, tiles, channels, LANES), F32),
             pltpu.VMEM((2, 2, channels, LANES), F32),
         ],
-    )(nb, srows, sstrip, scorner, pixel_slot, lat_kernel, lon_kernel, damping, here)
+    )(nb, srows, sstrip, scorner, pixel_slot, lat_kernel.T, lon_kernel.T, damping, here)
     return back_field, residual
 
 

time: 112 us -> 86.4 us (0.77)
  Pallas kernels: 107 us -> 85 us
  local copies, waits for them, and re-layouts: 3.34 us -> 0.61 us
    pallas_call x1, Pallas kernels: 41.2 us -> 29.9 us  [local(): pl.pallas_call(functools.partial(adjoint_kernel, lat_count, lon_count), o...]
    pallas_call x1, Pallas kernels: 66.2 us -> 55.1 us  [local(): pl.pallas_call(functools.partial(forward_kernel, lat_count, lon_count), o...]
    unnamed x5 -> x3, local copies, waits for them, and re-layouts: 3.34 us -> 0.61 us
where the time goes in v1:
time: 86.4 us; the launch traced here: 86.3 us
  Pallas kernels  85 us (98%)
    pallas_call x1, Pallas kernels, local(): pl.pallas_call(functools.partial(forward_kernel, lat_count, lon_count), o...  55.1 us
    pallas_call x1, Pallas kernels, local(): pl.pallas_call(functools.partial(adjoint_kernel, lat_count, lon_count), o...  29.9 us

profile of v1, /device:TPU:0, one launch (start us, length us, event | category | flops | bytes accessed | tf_op | source)
XLA Modules:
  0.0 86.3 jit_solution(8998253121355525788)
XLA Ops:
  0.6 55.1 %shard_map.86 = (f32[24,256]{1,0:T(8,128)}, f32[32,3,3,1,128]{4,3,2,1,0:T(1,128)}, s32[2,8,256]{2,1,0:T(8,128)}, f32[2,4,8,128]{3,2,1,0:T(8,128)}, f32[2,2,8,128]{3,2,1,0:T(8,128)}) custom-call(f32[24,64,256]{2,1,0:T(8,128)} %x_ref.1, f32[5,24]{1,0:T(8,128)} %bitcast.3, f32[5,24]{1,0:T(8,128)} %bitcast.5, f32[4,24]{1,0:T(4,128)} %damp_ref.3, ...), custom_call_target="tpu_custom_call" | custom-call | tf_op jit(solution)/shard_map/pallas_call | solution.py:475
  55.8 0.0 copy-start
  55.8 29.9 %shard_map.87 = f32[24,64,256]{2,1,0:T(8,128)} custom-call(f32[32,3,3,1,128]{4,3,2,1,0:T(1,128)} %get-tuple-element.7.nb_ref, s32[2,8,256]{2,1,0:T(8,128)} %get-tuple-element.8.srows_ref, f32[2,4,8,128]{3,2,1,0:T(8,128)} %get-tuple-element.9.sstrip_ref, f32[2,2,8,128]{3,2,1,0:T(8,128)} %get-tuple-element.10.scorner_ref, s32[64,256]{1,0:T(8,128)} %slot_ref.3, ...), custom_call_target="tpu_custom_call" | custom-call | tf_op jit(solution)/shard_map/pallas_call | solution.py:506
  85.6 0.0 copy-done
  85.6 0.6 copy.10
Async XLA Ops:
  55.8 29.9 %copy-start = (f32[24,256]{1,0:T(8,128)S(1)}, f32[24,256]{1,0:T(8,128)}, u32[]{:S(2)}) copy-start(f32[24,256]{1,0:T(8,128)} %get-tuple-element.15) | copy-start | bytes 73732

commit v2 on v1

--- a/solution.py
+++ b/solution.py
@@ -113,7 +113,13 @@
                 keep_lon(top + BLOCK + 2 + j, g, ahead[j])
         return 0
 
-    lax.fori_loop(0, blocks - 1, step, 0)
+    def two_steps(i, _):
+        step(2 * i, 0)
+        return step(2 * i + 1, 0)
+
+    lax.fori_loop(0, (blocks - 1) // 2, two_steps, 0)
+    if (blocks - 1) % 2:
+        step(blocks - 2, 0)
     for g in groups:
         lat(first + (blocks - 1) * BLOCK, g)
 
@@ -314,12 +320,15 @@
 
     ids = slot_ids(devices, cols)
 
-    def add_row(row, total):
-        block = stacked(done[HALO + row, :, 0:cols], LANES)
-        hot = one_hot(slot_ref[pl.ds(row, 1), :], ids)
-        return total + lax.dot_general(hot, block, NT, preferred_element_type=F32)
-
-    sums = lax.fori_loop(0, rows, add_row, jnp.zeros((CAP * devices, LANES), F32))
+    def add_rows(i, total):
+        for j in range(4):
+            row = 4 * i + j
+            block = stacked(done[HALO + row, :, 0:cols], LANES)
+            hot = one_hot(slot_ref[pl.ds(row, 1), :], ids)
+            total = total + lax.dot_general(hot, block, NT, preferred_element_type=F32)
+        return total
+
+    sums = lax.fori_loop(0, rows // 4, add_rows, jnp.zeros((CAP * devices, LANES), F32))
     sums = sums + pltpu.roll(sums, LANES - 32, 1) + pltpu.roll(sums, LANES - 64, 1)
     lane_d = lax.broadcasted_iota(jnp.int32, (devices, LANES), 1)
     sums = jnp.where(lane_d < 64, sums[:devices], pltpu.roll(sums[devices:], 64, 1))
@@ -429,11 +438,13 @@
             )
     ids = slot_ids(devices, cols)
 
-    def own(row, _):
-        buf_a[HALO + row, :, 0:cols] = mix(mixers[1, 1], one_hot(slot_ref[pl.ds(row, 1), :], ids))
-        return 0
-
-    lax.fori_loop(0, rows, own, 0)
+    def own(i, _):
+        made = [mix(mixers[1, 1], one_hot(slot_ref[pl.ds(4 * i + j, 1), :], ids)) for j in range(4)]
+        for j in range(4):
+            buf_a[HALO + 4 * i + j, :, 0:cols] = made[j]
+        return 0
+
+    lax.fori_loop(0, rows // 4, own, 0)
 
     def ghost(e, _):
         for v in range(2):

time: 86.4 us -> 70.6 us (0.82)
  Pallas kernels: 85 us -> 69.1 us
    pallas_call x1, Pallas kernels: 55.1 us -> 46.9 us  [local(): pl.pallas_call(functools.partial(forward_kernel, lat_count, lon_count), o...]
    pallas_call x1, Pallas kernels: 29.9 us -> 22.2 us  [local(): pl.pallas_call(functools.partial(adjoint_kernel, lat_count, lon_count), o...]
where the time goes in v2:
time: 70.6 us; the launch traced here: 70.4 us
  Pallas kernels  69.1 us (98%)
    pallas_call x1, Pallas kernels, local(): pl.pallas_call(functools.partial(forward_kernel, lat_count, lon_count), o...  46.9 us
    pallas_call x1, Pallas kernels, local(): pl.pallas_call(functools.partial(adjoint_kernel, lat_count, lon_count), o...  22.2 us

profile of v2, /device:TPU:0, one launch (start us, length us, event | category | flops | bytes accessed | tf_op | source)
XLA Modules:
  0.0 70.4 jit_solution(11585764296334492334)
XLA Ops:
  0.6 46.9 %shard_map.86 = (f32[24,256]{1,0:T(8,128)}, f32[32,3,3,1,128]{4,3,2,1,0:T(1,128)}, s32[2,8,256]{2,1,0:T(8,128)}, f32[2,4,8,128]{3,2,1,0:T(8,128)}, f32[2,2,8,128]{3,2,1,0:T(8,128)}) custom-call(f32[24,64,256]{2,1,0:T(8,128)} %x_ref.1, f32[5,24]{1,0:T(8,128)} %bitcast.3, f32[5,24]{1,0:T(8,128)} %bitcast.5, f32[4,24]{1,0:T(4,128)} %damp_ref.3, ...), custom_call_target="tpu_custom_call" | custom-call | tf_op jit(solution)/shard_map/pallas_call | solution.py:486
  47.6 0.0 copy-start
  47.6 22.2 %shard_map.87 = f32[24,64,256]{2,1,0:T(8,128)} custom-call(f32[32,3,3,1,128]{4,3,2,1,0:T(1,128)} %get-tuple-element.7.nb_ref, s32[2,8,256]{2,1,0:T(8,128)} %get-tuple-element.8.srows_ref, f32[2,4,8,128]{3,2,1,0:T(8,128)} %get-tuple-element.9.sstrip_ref, f32[2,2,8,128]{3,2,1,0:T(8,128)} %get-tuple-element.10.scorner_ref, s32[64,256]{1,0:T(8,128)} %slot_ref.3, ...), custom_call_target="tpu_custom_call" | custom-call | tf_op jit(solution)/shard_map/pallas_call | solution.py:517
  69.8 0.0 copy-done
  69.8 0.6 copy.10
Async XLA Ops:
  47.6 22.2 %copy-start = (f32[24,256]{1,0:T(8,128)S(1)}, f32[24,256]{1,0:T(8,128)}, u32[]{:S(2)}) copy-start(f32[24,256]{1,0:T(8,128)} %get-tuple-element.15) | copy-start | bytes 73732
